TPU v7x, 256 devices: a whole 4x4x8 slice. The times are simulated.
256 devices in a mesh: seq: 64 (over z, y, core), tensor: 4 (over x).
Axes of the slice: x: 4, y: 4, z: 8, core: 2. Of those that a mesh axis runs over, the one named last changes fastest.
Arguments:
- tokens: bfloat16 [8192, 1536], P('seq', 'tensor'), may hold values from -6 to 6
- attn_gain: float32 [1536], replicated, may hold values from 0.5 to 1.5
- q_weight: bfloat16 [1536, 1536], P(None, 'tensor'), may hold values from -0.15625 to 0.15625
- key_matrix: bfloat16 [1536, 512], P(None, 'tensor'), may hold values from -0.15625 to 0.15625
- value_matrix: bfloat16 [1536, 512], P(None, 'tensor'), may hold values from -0.15625 to 0.15625
- o_weight: bfloat16 [1536, 1536], P('tensor'), may hold values from -0.625 to 0.625
- moe_gain: float32 [1536], replicated, may hold values from 0.5 to 1.5
- gate_weight: bfloat16 [64, 1536, 512], P('seq', None, 'tensor'), may hold values from -0.15625 to 0.15625
- up_weight: bfloat16 [64, 1536, 512], P('seq', None, 'tensor'), may hold values from -0.15625 to 0.15625
- down_weight: bfloat16 [64, 512, 1536], P('seq', 'tensor'), may hold values from -0.25 to 0.25
- key_page_pool: bfloat16 [4096, 128, 512], P('seq', None, 'tensor'), may hold values from -140 to 140
- value_page_pool: bfloat16 [4096, 128, 512], P('seq', None, 'tensor'), may hold values from -6 to 6
- cache_lens: int32 [64], P('seq'), may hold values from 1 to 8192, as said below
- page_table: int32 [64, 64], P('seq'), may hold values from 0 to 63, each once within a row
- routes: int32 [8192, 8], P('seq'), may hold values from 0 to 39, all different within a row; in each aligned block of 128 rows (0 to 127, 128 to 255, ...) at most 32 rows name the same one
- route_gates: float32 [8192, 8], P('seq'), may hold values from 0.1 to 1
Outputs:
- mixed: bfloat16 [8192, 1536], P('seq', 'tensor')
Inputs may be any that keep to these rules, and one draw needn't show every extreme that they name: `cache_lens`: some request has exactly 8192 cached tokens in every draw. `page_table`: each row is a permutation of 0 .. 63. `routes`: each row names 8 different experts. Among the 128 rows of one request no expert is named more than 32 times, a bound that some block reaches.
All inputs are finite; a program needn't handle non-finite values.
Results may differ from a plain program's by a relative error of at most 0.017.
The roundings to bfloat16 on the way count: a program that leaves them out, or rounds other values in their place, can miss the bound.
Values may be sent and summed in bfloat16 or wider, within the bound.
A program may use at most 128 MiB of HBM per device.

v0:
```python
import jax
import jax.numpy as jnp
from jax import lax
from jax.sharding import PartitionSpec as P

HEAD_SIZE = 64
CAP = 32
NORM_EPSILON = 1e-06
MASKED_SCORE = -1e30


def norm_rows(field, gain_row):
    widened = field.astype(jnp.float32)
    return (
        widened
        * lax.rsqrt(jnp.mean(widened * widened, axis=1, keepdims=True) + NORM_EPSILON)
        * gain_row
    )


def apply_rotary(field, token_places):
    head_dim = field.shape[-1]
    half_dim = head_dim // 2
    frequency = 10000.0 ** (-2.0 * jnp.arange(half_dim, dtype=jnp.float32) / head_dim)
    phase_angle = token_places[:, None, None] * frequency
    cosine = jnp.cos(phase_angle)
    sine_part = jnp.sin(phase_angle)
    lower_half = field[..., :half_dim]
    upper_half = field[..., half_dim:]
    return jnp.concatenate(
        [
            lower_half * cosine - upper_half * sine_part,
            upper_half * cosine + lower_half * sine_part,
        ],
        axis=-1,
    )


def attend(
    query_rows, incoming_keys, incoming_values, key_pool, value_pool, table_row, cached_length
):
    row_count = query_rows.shape[0]
    kv_count = incoming_keys.shape[1]
    head_dim = incoming_keys.shape[2]
    page_count = key_pool.shape[0]
    page_rows = key_pool.shape[1]
    per_block = min(page_count, max(1, 512 // page_rows))
    block_count = page_count // per_block
    block_span = per_block * page_rows
    score_scale = head_dim ** (-0.5)
    causal = jnp.arange(row_count)[None, :] <= jnp.arange(row_count)[:, None]
    fresh_scores = (
        jnp.einsum("tgjd,sgd->gjts", query_rows, incoming_keys, preferred_element_type=jnp.float32)
        * score_scale
    )
    fresh_scores = jnp.where(causal, fresh_scores, MASKED_SCORE)

    def load_block(pool, block_id):
        page_index = lax.dynamic_slice_in_dim(table_row, block_id * per_block, per_block)
        return pool[page_index].reshape(block_span, kv_count, head_dim)

    def weighted(scores, values, row_best):
        weights = jnp.exp(scores - row_best[..., None])
        weights_b = weights.astype(jnp.bfloat16)
        return (
            jnp.sum(weights, axis=-1),
            jnp.einsum("gjts,sgd->gjtd", weights_b, values, preferred_element_type=jnp.float32),
        )

    def block_step(block_id, carried):
        old_best, old_total, old_mix = carried
        block_keys = load_block(key_pool, block_id)
        scores = (
            jnp.einsum("tgjd,sgd->gjts", query_rows, block_keys, preferred_element_type=jnp.float32)
            * score_scale
        )
        visible = block_id * block_span + jnp.arange(block_span, dtype=jnp.int32) < cached_length
        scores = jnp.where(visible, scores, MASKED_SCORE)
        new_best = jnp.maximum(old_best, jnp.max(scores, axis=-1))
        rescale = jnp.exp(old_best - new_best)
        block_total, block_mix = weighted(scores, load_block(value_pool, block_id), new_best)
        return (
            new_best,
            old_total * rescale + block_total,
            old_mix * rescale[..., None] + block_mix,
        )

    first_best = jnp.max(fresh_scores, axis=-1)
    first_total, first_mix = weighted(fresh_scores, incoming_values, first_best)
    _, denominator, mixture = lax.fori_loop(
        0, block_count, block_step, (first_best, first_total, first_mix)
    )
    result = mixture / denominator[..., None]
    return jnp.transpose(result, (2, 0, 1, 3)).reshape(row_count, -1).astype(jnp.bfloat16)


def slot_places(routes, capacity, expert_total):
    flat_routes = routes.reshape(-1)
    route_hits = (
        flat_routes[:, None] == jnp.arange(expert_total, dtype=jnp.int32)[None, :]
    ).astype(jnp.int32)
    earlier = jnp.cumsum(route_hits, axis=0) - route_hits
    return flat_routes * capacity + jnp.sum(earlier * route_hits, axis=1)


def pack_rows(moe_in, slot_place, capacity, expert_total):
    top_count = slot_place.shape[0] // moe_in.shape[0]
    token_rows = jnp.arange(slot_place.shape[0], dtype=jnp.int32) // top_count
    outgoing = jnp.zeros((expert_total * capacity, moe_in.shape[1]), moe_in.dtype)
    outgoing = outgoing.at[slot_place].set(moe_in[token_rows])
    return outgoing.reshape(expert_total, capacity, moe_in.shape[1])


def finish_partial(gate_act, up_act, down_weight, slot_place, route_gates, residual_cols):
    row_count = residual_cols.shape[0]
    hidden = (jax.nn.silu(gate_act) * up_act).astype(jnp.bfloat16)
    expert_out = jnp.einsum(
        "secf,efd->secd", hidden, down_weight, preferred_element_type=jnp.float32
    )
    expert_cols = lax.psum_scatter(
        expert_out.astype(jnp.bfloat16), "tensor", scatter_dimension=3, tiled=True
    )
    col_count = expert_cols.shape[3]
    returned = lax.all_to_all(
        expert_cols.reshape(-1, expert_cols.shape[2], col_count),
        "seq",
        split_axis=0,
        concat_axis=0,
        tiled=True,
    )
    picked = (
        returned.reshape(-1, col_count)[slot_place].astype(jnp.float32)
        * route_gates.reshape(-1)[:, None]
    )
    expert_mix = jnp.sum(picked.reshape(row_count, -1, col_count), axis=1)
    return (residual_cols.astype(jnp.float32) + expert_mix).astype(jnp.bfloat16)


def shards(
    tokens,
    attn_gain,
    q_weight,
    key_matrix,
    value_matrix,
    o_weight,
    moe_gain,
    gate_weight,
    up_weight,
    down_weight,
    key_page_pool,
    value_page_pool,
    cache_lens,
    page_table,
    routes,
    route_gates,
):
    row_count = tokens.shape[0]
    col_count = tokens.shape[1]
    group_count = lax.axis_size("seq")
    tensor_index = lax.axis_index("tensor")
    column_start = tensor_index * col_count
    local_experts = gate_weight.shape[0]
    expert_total = local_experts * group_count
    whole = lax.all_gather(tokens, "tensor", axis=1, tiled=True)
    normed = norm_rows(whole, attn_gain).astype(jnp.bfloat16)
    head_count = q_weight.shape[1] // HEAD_SIZE
    kv_count = key_matrix.shape[1] // HEAD_SIZE
    token_places = (cache_lens[0] + jnp.arange(row_count, dtype=jnp.int32)).astype(jnp.float32)
    query_rows = jnp.dot(normed, q_weight, preferred_element_type=jnp.float32).reshape(
        row_count, head_count, HEAD_SIZE
    )
    query_rows = (
        apply_rotary(query_rows, token_places)
        .astype(jnp.bfloat16)
        .reshape(row_count, kv_count, head_count // kv_count, HEAD_SIZE)
    )
    incoming_keys = jnp.dot(normed, key_matrix, preferred_element_type=jnp.float32).reshape(
        row_count, kv_count, HEAD_SIZE
    )
    incoming_keys = apply_rotary(incoming_keys, token_places).astype(jnp.bfloat16)
    incoming_values = (
        jnp.dot(normed, value_matrix, preferred_element_type=jnp.float32)
        .reshape(row_count, kv_count, HEAD_SIZE)
        .astype(jnp.bfloat16)
    )
    attended = attend(
        query_rows,
        incoming_keys,
        incoming_values,
        key_page_pool,
        value_page_pool,
        page_table[0],
        cache_lens[0],
    )
    partial_value = jnp.dot(attended, o_weight, preferred_element_type=jnp.float32)
    slot_place = slot_places(routes, CAP, expert_total)
    summed = lax.psum(partial_value.astype(jnp.bfloat16), "tensor").astype(jnp.float32)
    residual = (whole.astype(jnp.float32) + summed).astype(jnp.bfloat16)
    moe_in = norm_rows(residual, moe_gain).astype(jnp.bfloat16)
    residual_cols = lax.dynamic_slice_in_dim(residual, column_start, col_count, 1)
    received = lax.all_to_all(
        pack_rows(moe_in, slot_place, CAP, expert_total),
        "seq",
        split_axis=0,
        concat_axis=0,
        tiled=True,
    )
    received = received.reshape(group_count, local_experts, CAP, -1)
    gate_act = jnp.einsum(
        "secd,edf->secf", received, gate_weight, preferred_element_type=jnp.float32
    )
    up_act = jnp.einsum("secd,edf->secf", received, up_weight, preferred_element_type=jnp.float32)
    return finish_partial(gate_act, up_act, down_weight, slot_place, route_gates, residual_cols)


def solution(mesh):
    in_specs = (
        P("seq", "tensor"),
        P(),
        P(None, "tensor"),
        P(None, "tensor"),
        P(None, "tensor"),
        P("tensor", None),
        P(),
        P("seq", None, "tensor"),
        P("seq", None, "tensor"),
        P("seq", "tensor", None),
        P("seq", None, "tensor"),
        P("seq", None, "tensor"),
        P("seq"),
        P("seq", None),
        P("seq", None),
        P("seq", None),
    )
    out_specs = P("seq", "tensor")
    return jax.shard_map(shards, mesh=mesh, in_specs=in_specs, out_specs=out_specs, check_vma=False)
```

profile of v0, /device:TPU:1, one launch (start us, length us, event | category | flops | bytes accessed | tf_op | source)
XLA Modules:
  0.0 581.9 jit_solution(12883326083600127530)
XLA Ops:
  6.6 12.0 %all_gather.3 = bf16[128,1536]{1,0:T(8,128)(2,1)S(1)} all-gather(bf16[128,384]{1,0:T(8,128)(2,1)} %param.18), channel_id=1, replica_groups=mesh['seq'=64,'tensor'=4] {'tensor'}, dimensions={1}, use_global_device_ids=true | all-gather | bytes 491520 | tf_op jit(solution)/shard_map/all_gather | solution.py:164
  23.0 106.6 %while.17 = (s32[]{:T(128)}, f32[2,3,128]{2,1,0:T(4,128)S(1)}, f32[2,3,128]{2,1,0:T(4,128)S(1)}, f32[2,3,128,64]{2,3,1,0:T(8,128)S(1)}, s32[]{:T(128)}, /*index=...) while((s32[]{:T(128)}, f32[2,3,128]{2,1,0:T(4,128)S(1)}, ...), condition=%wide.region_6.7_spmd, body=%wide.region_3.6_spmd.sunk | while | flops 103517712 | bytes 7099675 | solution.py:90
  26.8 2.2 gather_fusion.1
  33.5 2.2 gather_fusion.1
  40.1 2.2 gather_fusion.1
  46.8 2.2 gather_fusion.1
  53.5 2.2 gather_fusion.1
  60.1 2.2 gather_fusion.1
  66.8 2.2 gather_fusion.1
  73.5 2.2 gather_fusion.1
  80.1 2.2 gather_fusion.1
  86.8 2.2 gather_fusion.1
  93.4 2.2 gather_fusion.1
  100.1 2.2 gather_fusion.1
  106.8 2.2 gather_fusion.1
  113.4 2.2 gather_fusion.1
  120.1 2.2 gather_fusion.1
  126.7 2.2 gather_fusion.1
  131.3 18.0 %reduce-window.6 = s32[64,8,128]{2,1,0:T(8,128)S(1)} reduce-window(s32[64,8,128]{2,1,0:T(8,128)S(1)} %fusion.33, s32[]{:T(128)} %constant.103.clone.1), window={size=1x1x128 pad=0_0x0_0x127_0}, to_apply=%region_8.9 | reduce-window | flops 8323072 | bytes 524292 | tf_op jit(solution)/shard_map/reduce-window
  150.2 30.9 %all-reduce.2.cloned.1.call-done = bf16[128,1536]{1,0:T(8,128)(2,1)} async-done(((bf16[128,1536]{1,0:T(8,128)(2,1)}), bf16[128,1536]{1,0:T(8,128)(2,1)}) %all-reduce.2.cloned.1.call-update) | async-done | bytes 393232 | tf_op jit(solution)/shard_map/psum | solution.py:197
  182.6 19.7 %scatter_custom_fusion = bf16[2048,1536]{1,0:T(8,128)(2,1)} fusion(s32[1024]{0:T(1024)S(1)} %bitcast.160, bf16[128,1536]{1,0:T(8,128)(2,1)S(1)} %fusion.18, s32[1024]{0:T(1024)S(1)} %broadcast_clamp_fusion.1, bf16[]{:T(256)} %constant.115.clone.1), kind=kCustom, calls=%fused_computation.21 | custom fusion | bytes 6291458 | tf_op jit(solution)/shard_map/scatter | solution.py:110
  202.3 152.4 %all_to_all.10 = bf16[64,32,1536]{2,1,0:T(8,128)(2,1)S(1)} all-to-all(bf16[64,32,1536]{2,1,0:T(8,128)(2,1)} %bitcast.146), channel_id=1, replica_groups=mesh['seq'=64,'tensor'=4] {'seq'}, dimensions={0} | all-to-all | bytes 12582912 | tf_op jit(solution)/shard_map/all_to_all | solution.py:201
  354.7 2.7 copy-done.2
  359.2 11.8 %convert_bitcast_fusion = bf16[64,1,32,1536]{3,2,0,1:T(8,128)(2,1)} fusion(bf16[64,32,1536]{2,1,0:T(8,128)(2,1)} %copy-done.2, f32[64,1,32,128]{3,2,0,1:T(8,128)S(1)} %convolution_bitcast_fusion.1, bf16[1,128,1536]{2,1,0:T(8,128)(2,1)S(1)} %copy-done.6, bf16[1,1536,128]{2,1,0:T(8,128)(2,1)S(1)} %copy-done.7), kind=kOutput, calls=%fused_computation.20 | convolution fusion | flops 1615331328 | bytes 14417920 | tf_op jit(solution)/shard_map/secf,efd->secd/dot_general | solution.py:117
  371.0 33.7 %copy.55 = bf16[64,1,32,1536]{2,0,1,3:T(8,128)(2,1)} copy(bf16[64,1,32,1536]{3,2,0,1:T(8,128)(2,1)} %convert_bitcast_fusion) | data formatting | bytes 12582912
  404.7 33.1 %reshape.310 = bf16[1536,2048]{1,0:T(8,128)(2,1)} reshape(bf16[1536,1,64,32]{3,2,1,0:T(8,128)(2,1)} %bitcast.144) | data formatting | bytes 12582912
  437.8 63.6 %reduce-scatter.4.cloned.1.call-done = bf16[384,2048]{1,0:T(8,128)(2,1)} async-done(((bf16[1536,2048]{1,0:T(8,128)(2,1)}), bf16[384,2048]{1,0:T(8,128)(2,1)}) %reduce-scatter.4.cloned.1.call-update) | async-done | bytes 1572880
  501.4 8.4 %reshape.311 = bf16[384,1,64,32]{3,2,1,0:T(8,128)(2,1)} reshape(bf16[384,2048]{1,0:T(8,128)(2,1)} %reduce-scatter.4.cloned.1.call-done) | data formatting | bytes 3145728
  509.7 8.7 %copy.56 = bf16[64,1,32,384]{3,2,0,1:T(8,128)(2,1)} copy(bf16[64,1,32,384]{2,0,1,3:T(8,128)(2,1)} %bitcast.147) | data formatting | bytes 3145728
  518.5 10.8 %all-to-all-start.1 = ((bf16[64,32,384]{2,1,0:T(8,128)(2,1)}), bf16[64,32,384]{2,1,0:T(8,128)(2,1)S(1)}, u32[]{:S(2)}, u32[]{:S(2)}) async-start(bf16[64,32,384]{2,1,0:T(8,128)(2,1)} %bitcast.148), calls=%async_computation.1 | async-start | bytes 3145728 | tf_op jit(solution)/shard_map/all_to_all | solution.py:124
  530.0 38.2 %all-to-all-done.1 = bf16[64,32,384]{2,1,0:T(8,128)(2,1)S(1)} async-done(((bf16[64,32,384]{2,1,0:T(8,128)(2,1)}), bf16[64,32,384]{2,1,0:T(8,128)(2,1)S(1)}, u32[]{:S(2)}, u32[]{:S(2)}) %all-to-all-start.1) | async-done | bytes 1572896 | tf_op jit(solution)/shard_map/all_to_all | solution.py:124
  568.2 3.9 gather_fusion.2
  (301 shorter events, 83.3 us)
Async XLA Ops:
  6.5 123.1 %copy-start = (bf16[384,1536]{1,0:T(8,128)(2,1)S(1)}, bf16[384,1536]{1,0:T(8,128)(2,1)}, u32[]{:S(2)}) copy-start(bf16[384,1536]{1,0:T(8,128)(2,1)} %param.23) | copy-start | bytes 3538948
  6.5 14.9 %copy-start.9 = (f32[1536]{0:T(1024)S(1)}, f32[1536]{0:T(1024)}, u32[]{:S(2)}) copy-start(f32[1536]{0:T(1024)} %param.19) | copy-start | bytes 18436
  6.5 14.9 %copy-start.12 = (bf16[1536,128]{1,0:T(8,128)(2,1)S(1)}, bf16[1536,128]{1,0:T(8,128)(2,1)}, u32[]{:S(2)}) copy-start(bf16[1536,128]{1,0:T(8,128)(2,1)} %param.21) | copy-start | bytes 1179652
  6.5 15.5 %copy-start.13 = (bf16[1536,128]{1,0:T(8,128)(2,1)S(1)}, bf16[1536,128]{1,0:T(8,128)(2,1)}, u32[]{:S(2)}) copy-start(bf16[1536,128]{1,0:T(8,128)(2,1)} %param.22) | copy-start | bytes 1179652
  6.5 174.6 %all-reduce.2.cloned.1.call-start = ((), (), s32[]{:S(2)}) async-start(), calls=%async_computation.3 | async-start | bytes 786432 | tf_op jit(solution)/shard_map/psum | solution.py:197
  18.7 3.7 copy-start.3
  21.4 1.5 copy-start.15
  129.6 1.5 copy-start.8
  129.6 51.6 %copy-start.4 = (bf16[128,1536]{1,0:T(8,128)(2,1)S(1)}, bf16[128,1536]{1,0:T(8,128)(2,1)}, u32[]{:S(2)}) copy-start(bf16[128,1536]{1,0:T(8,128)(2,1)} %copy-done.3) | copy-start | bytes 1179652
  130.8 51.6 %copy-start.10 = (f32[1536]{0:T(1024)S(1)}, f32[1536]{0:T(1024)}, u32[]{:S(2)}) copy-start(f32[1536]{0:T(1024)} %param.24) | copy-start | bytes 18436
  130.8 370.6 %reduce-scatter.4.cloned.1.call-start = ((), (), s32[]{:S(2)}) async-start(), calls=%async_computation.4 | async-start | bytes 7864320
  182.4 19.9 %copy-start.5 = (bf16[128,1536]{1,0:T(8,128)(2,1)}, bf16[128,1536]{1,0:T(8,128)(2,1)S(1)}, u32[]{:S(2)}) copy-start(bf16[128,1536]{1,0:T(8,128)(2,1)S(1)} %get-tuple-element.183) | copy-start | bytes 1179652
  202.3 155.0 %copy-start.14 = (bf16[1,1536,128]{2,1,0:T(8,128)(2,1)S(1)}, bf16[1,1536,128]{2,1,0:T(8,128)(2,1)}, u32[]{:S(2)}) copy-start(bf16[1,1536,128]{2,1,0:T(8,128)(2,1)} %param.25) | copy-start | bytes 1179652
  354.7 2.7 copy-start.2
  357.4 1.8 copy-start.6
  357.4 1.8 copy-start.7
  518.5 10.8 %copy-start.11 = (f32[128,8]{0,1:T(8,128)S(1)}, f32[128,8]{0,1:T(8,128)}, u32[]{:S(2)}) copy-start(f32[128,8]{0,1:T(8,128)} %param.33) | copy-start | bytes 12292
  518.5 49.8 %all-to-all-start.1 = ((bf16[64,32,384]{2,1,0:T(8,128)(2,1)}), bf16[64,32,384]{2,1,0:T(8,128)(2,1)S(1)}, u32[]{:S(2)}, u32[]{:S(2)}) async-start(bf16[64,32,384]{2,1,0:T(8,128)(2,1)} %bitcast.148), calls=%async_computation.1 | async-start | bytes 3145728 | tf_op jit(solution)/shard_map/all_to_all | solution.py:124
  568.2 6.9 %copy-start.1 = (bf16[384,1536]{1,0:T(8,128)(2,1)S(1)}, bf16[384,1536]{1,0:T(8,128)(2,1)}, u32[]{:S(2)}) copy-start(bf16[384,1536]{1,0:T(8,128)(2,1)} %param.23) | copy-start | bytes 3538948
Sparse Core Ops, SparseCore 0:
  130.9 50.2 all-reduce.1
  437.9 63.4 reduce-scatter.3
where the time goes:
time: 585 us; the launch traced here: 582 us
  local copies, waits for them, and re-layouts  187 us (32%)
  blocking collectives  164 us (28%)
  waiting for transfers between devices  133 us (23%)
  other arithmetic  38.9 us (7%)
  matrix products  31.2 us (5%)
  between operations  14.4 us (2%)
  starting transfers between devices  11 us (2%)
    all_to_all x1, blocking collectives, shards(): lax.all_to_all(pack_rows(moe_in, slot_place, CAP, expert_total), 'seq', s...  152 us
    unnamed x38, local copies, waits for them, and re-layouts  87.4 us
    gather x64, local copies, waits for them, and re-layouts, load_block(): return pool[page_index].reshape(block_span, kv_count, head_dim)  73.8 us
    unnamed x3, waiting for transfers between devices  63.6 us
    all_to_all x1, waiting for transfers between devices, finish_partial(): lax.all_to_all(expert_cols.reshape(-1, expert_cols.shape[2], col_count),...  38.2 us
    psum x1, waiting for transfers between devices, shards(): lax.psum(partial_value.astype(jnp.bfloat16), 'tensor').astype(jnp.float32)  30.9 us
    scatter x1, local copies, waits for them, and re-layouts, pack_rows(): outgoing = outgoing.at[slot_place].set(moe_in[token_rows])  19.7 us
    another operation x5, other arithmetic  18.2 us
  transfers between devices with their start and end apart: 3, of which 3 were waited for; matrix products, arithmetic and copies ran while one was open for 3% of the time, Pallas kernels for 0%

commit v1 on v0

--- a/solution.py
+++ b/solution.py
@@ -194,7 +194,9 @@
     )
     partial_value = jnp.dot(attended, o_weight, preferred_element_type=jnp.float32)
     slot_place = slot_places(routes, CAP, expert_total)
-    summed = lax.psum(partial_value.astype(jnp.bfloat16), "tensor").astype(jnp.float32)
+    summed = jnp.sum(lax.all_gather(partial_value.astype(jnp.bfloat16), "tensor"), axis=0).astype(
+        jnp.float32
+    )
     residual = (whole.astype(jnp.float32) + summed).astype(jnp.bfloat16)
     moe_in = norm_rows(residual, moe_gain).astype(jnp.bfloat16)
     residual_cols = lax.dynamic_slice_in_dim(residual, column_start, col_count, 1)

time: 585 us -> 567 us (0.969)
  waiting for transfers between devices: 133 us -> 116 us
    psum x1 -> x0, waiting for transfers between devices: 30.9 us -> none  [shards(): lax.psum(partial_value.astype(jnp.bfloat16), 'tensor').astype(jnp.float32)]
    all_gather x0 -> x1, waiting for transfers between devices: none -> 14.7 us  [shards(): lax.all_gather(partial_value.astype(jnp.bfloat16), 'tensor')]
  transfers between devices with their start and end apart: 3 -> 3, of which waited for: 3 -> 3; matrix products, arithmetic and copies ran while one was open for 3% -> 4% of each run, Pallas kernels for 0% -> 0%
where the time goes in v1:
time: 567 us; the launch traced here: 564 us
  local copies, waits for them, and re-layouts  187 us (33%)
  blocking collectives  162 us (29%)
  waiting for transfers between devices  116 us (20%)
  other arithmetic  39.6 us (7%)
  matrix products  31.2 us (6%)
  between operations  14.4 us (3%)
  starting transfers between devices  11 us (2%)
    all_to_all x1, blocking collectives, shards(): lax.all_to_all(pack_rows(moe_in, slot_place, CAP, expert_total), 'seq', s...  150 us
    unnamed x38, local copies, waits for them, and re-layouts  87.4 us
    gather x64, local copies, waits for them, and re-layouts, load_block(): return pool[page_index].reshape(block_span, kv_count, head_dim)  73.8 us
    unnamed x3, waiting for transfers between devices  63.1 us
    all_to_all x1, waiting for transfers between devices, finish_partial(): lax.all_to_all(expert_cols.reshape(-1, expert_cols.shape[2], col_count),...  38.2 us
    scatter x1, local copies, waits for them, and re-layouts, pack_rows(): outgoing = outgoing.at[slot_place].set(moe_in[token_rows])  19.7 us
    another operation x5, other arithmetic  18.2 us
    all_gather x1, waiting for transfers between devices, shards(): lax.all_gather(partial_value.astype(jnp.bfloat16), 'tensor')  14.7 us
  transfers between devices with their start and end apart: 3, of which 3 were waited for; matrix products, arithmetic and copies ran while one was open for 4% of the time, Pallas kernels for 0%

profile of v1, /device:TPU:1, one launch (start us, length us, event | category | flops | bytes accessed | tf_op | source)
XLA Modules:
  0.0 563.8 jit_solution(12580785060182837813)
XLA Ops:
  6.6 12.0 %all_gather.9 = bf16[128,1536]{1,0:T(8,128)(2,1)S(1)} all-gather(bf16[128,384]{1,0:T(8,128)(2,1)} %param.18), channel_id=1, replica_groups=mesh['seq'=64,'tensor'=4] {'tensor'}, dimensions={1}, use_global_device_ids=true | all-gather | bytes 491520 | tf_op jit(solution)/shard_map/all_gather | solution.py:164
  23.0 106.6 %while.17 = (s32[]{:T(128)}, f32[2,3,128]{2,1,0:T(4,128)S(1)}, f32[2,3,128]{2,1,0:T(4,128)S(1)}, f32[2,3,128,64]{2,3,1,0:T(8,128)S(1)}, s32[]{:T(128)}, /*index=...) while((s32[]{:T(128)}, f32[2,3,128]{2,1,0:T(4,128)S(1)}, ...), condition=%wide.region_6.7_spmd, body=%wide.region_3.6_spmd.sunk | while | flops 103517712 | bytes 7099675 | solution.py:90
  26.8 2.2 gather_fusion.1
  33.5 2.2 gather_fusion.1
  40.1 2.2 gather_fusion.1
  46.8 2.2 gather_fusion.1
  53.5 2.2 gather_fusion.1
  60.1 2.2 gather_fusion.1
  66.8 2.2 gather_fusion.1
  73.5 2.2 gather_fusion.1
  80.1 2.2 gather_fusion.1
  86.8 2.2 gather_fusion.1
  93.4 2.2 gather_fusion.1
  100.1 2.2 gather_fusion.1
  106.8 2.2 gather_fusion.1
  113.4 2.2 gather_fusion.1
  120.1 2.2 gather_fusion.1
  126.7 2.2 gather_fusion.1
  131.4 18.0 %reduce-window.6 = s32[64,8,128]{2,1,0:T(8,128)S(1)} reduce-window(s32[64,8,128]{2,1,0:T(8,128)S(1)} %fusion.33, s32[]{:T(128)} %constant.104.clone.1), window={size=1x1x128 pad=0_0x0_0x127_0}, to_apply=%region_8.9 | reduce-window | flops 8323072 | bytes 524292 | tf_op jit(solution)/shard_map/reduce-window
  150.3 14.7 %all-gather.3.cloned.1.call-done = bf16[512,1536]{1,0:T(8,128)(2,1)} async-done(((bf16[128,1536]{1,0:T(8,128)(2,1)}), bf16[512,1536]{1,0:T(8,128)(2,1)}) %all-gather.3.cloned.1.call-update) | async-done | bytes 1572880 | tf_op jit(solution)/shard_map/all_gather | solution.py:197
  167.1 19.7 %scatter_custom_fusion = bf16[2048,1536]{1,0:T(8,128)(2,1)} fusion(s32[1024]{0:T(1024)S(1)} %bitcast.162, bf16[128,1536]{1,0:T(8,128)(2,1)S(1)} %fusion.18, s32[1024]{0:T(1024)S(1)} %broadcast_clamp_fusion.1, bf16[]{:T(256)} %constant.113.clone.1), kind=kCustom, calls=%fused_computation.21 | custom fusion | bytes 6291458 | tf_op jit(solution)/shard_map/scatter | solution.py:110
  186.8 150.3 %all_to_all.10 = bf16[64,32,1536]{2,1,0:T(8,128)(2,1)S(1)} all-to-all(bf16[64,32,1536]{2,1,0:T(8,128)(2,1)} %bitcast.147), channel_id=1, replica_groups=mesh['seq'=64,'tensor'=4] {'seq'}, dimensions={0} | all-to-all | bytes 12582912 | tf_op jit(solution)/shard_map/all_to_all | solution.py:203
  337.1 2.7 copy-done.2
  341.6 11.8 %convert_bitcast_fusion = bf16[64,1,32,1536]{3,2,0,1:T(8,128)(2,1)} fusion(bf16[64,32,1536]{2,1,0:T(8,128)(2,1)} %copy-done.2, f32[64,1,32,128]{3,2,0,1:T(8,128)S(1)} %convolution_bitcast_fusion.1, bf16[1,128,1536]{2,1,0:T(8,128)(2,1)S(1)} %copy-done.6, bf16[1,1536,128]{2,1,0:T(8,128)(2,1)S(1)} %copy-done.7), kind=kOutput, calls=%fused_computation.20 | convolution fusion | flops 1615331328 | bytes 14417920 | tf_op jit(solution)/shard_map/secf,efd->secd/dot_general | solution.py:117
  353.4 33.7 %copy.55 = bf16[64,1,32,1536]{2,0,1,3:T(8,128)(2,1)} copy(bf16[64,1,32,1536]{3,2,0,1:T(8,128)(2,1)} %convert_bitcast_fusion) | data formatting | bytes 12582912
  387.1 33.1 %reshape.311 = bf16[1536,2048]{1,0:T(8,128)(2,1)} reshape(bf16[1536,1,64,32]{3,2,1,0:T(8,128)(2,1)} %bitcast.145) | data formatting | bytes 12582912
  420.2 63.0 %reduce-scatter.4.cloned.1.call-done = bf16[384,2048]{1,0:T(8,128)(2,1)} async-done(((bf16[1536,2048]{1,0:T(8,128)(2,1)}), bf16[384,2048]{1,0:T(8,128)(2,1)}) %reduce-scatter.4.cloned.1.call-update) | async-done | bytes 1572880
  483.2 8.4 %reshape.312 = bf16[384,1,64,32]{3,2,1,0:T(8,128)(2,1)} reshape(bf16[384,2048]{1,0:T(8,128)(2,1)} %reduce-scatter.4.cloned.1.call-done) | data formatting | bytes 3145728
  491.6 8.7 %copy.56 = bf16[64,1,32,384]{3,2,0,1:T(8,128)(2,1)} copy(bf16[64,1,32,384]{2,0,1,3:T(8,128)(2,1)} %bitcast.148) | data formatting | bytes 3145728
  500.3 10.8 %all-to-all-start.1 = ((bf16[64,32,384]{2,1,0:T(8,128)(2,1)}), bf16[64,32,384]{2,1,0:T(8,128)(2,1)S(1)}, u32[]{:S(2)}, u32[]{:S(2)}) async-start(bf16[64,32,384]{2,1,0:T(8,128)(2,1)} %bitcast.149), calls=%async_computation.1 | async-start | bytes 3145728 | tf_op jit(solution)/shard_map/all_to_all | solution.py:124
  511.9 38.2 %all-to-all-done.1 = bf16[64,32,384]{2,1,0:T(8,128)(2,1)S(1)} async-done(((bf16[64,32,384]{2,1,0:T(8,128)(2,1)}), bf16[64,32,384]{2,1,0:T(8,128)(2,1)S(1)}, u32[]{:S(2)}, u32[]{:S(2)}) %all-to-all-start.1) | async-done | bytes 1572896 | tf_op jit(solution)/shard_map/all_to_all | solution.py:124
  550.1 3.9 gather_fusion.2
  (302 shorter events, 84.0 us)
Async XLA Ops:
  6.5 123.1 %copy-start = (bf16[384,1536]{1,0:T(8,128)(2,1)S(1)}, bf16[384,1536]{1,0:T(8,128)(2,1)}, u32[]{:S(2)}) copy-start(bf16[384,1536]{1,0:T(8,128)(2,1)} %param.23) | copy-start | bytes 3538948
  6.5 14.9 %copy-start.9 = (f32[1536]{0:T(1024)S(1)}, f32[1536]{0:T(1024)}, u32[]{:S(2)}) copy-start(f32[1536]{0:T(1024)} %param.19) | copy-start | bytes 18436
  6.5 14.9 %copy-start.12 = (bf16[1536,128]{1,0:T(8,128)(2,1)S(1)}, bf16[1536,128]{1,0:T(8,128)(2,1)}, u32[]{:S(2)}) copy-start(bf16[1536,128]{1,0:T(8,128)(2,1)} %param.21) | copy-start | bytes 1179652
  6.5 15.5 %copy-start.13 = (bf16[1536,128]{1,0:T(8,128)(2,1)S(1)}, bf16[1536,128]{1,0:T(8,128)(2,1)}, u32[]{:S(2)}) copy-start(bf16[1536,128]{1,0:T(8,128)(2,1)} %param.22) | copy-start | bytes 1179652
  6.5 158.5 %all-gather.3.cloned.1.call-start = ((), (), s32[]{:S(2)}) async-start(), calls=%async_computation.3 | async-start | bytes 1966080 | tf_op jit(solution)/shard_map/all_gather | solution.py:197
  18.7 3.7 copy-start.3
  21.4 1.5 copy-start.15
  129.6 1.5 copy-start.8
  130.8 352.4 %reduce-scatter.4.cloned.1.call-start = ((), (), s32[]{:S(2)}) async-start(), calls=%async_computation.4 | async-start | bytes 7864320
  131.4 35.3 %copy-start.4 = (bf16[128,1536]{1,0:T(8,128)(2,1)S(1)}, bf16[128,1536]{1,0:T(8,128)(2,1)}, u32[]{:S(2)}) copy-start(bf16[128,1536]{1,0:T(8,128)(2,1)} %copy-done.3) | copy-start | bytes 1179652
  149.7 17.2 %copy-start.10 = (f32[1536]{0:T(1024)S(1)}, f32[1536]{0:T(1024)}, u32[]{:S(2)}) copy-start(f32[1536]{0:T(1024)} %param.24) | copy-start | bytes 18436
  166.9 19.9 %copy-start.5 = (bf16[128,1536]{1,0:T(8,128)(2,1)}, bf16[128,1536]{1,0:T(8,128)(2,1)S(1)}, u32[]{:S(2)}) copy-start(bf16[128,1536]{1,0:T(8,128)(2,1)S(1)} %get-tuple-element.183) | copy-start | bytes 1179652
  186.8 152.9 %copy-start.14 = (bf16[1,1536,128]{2,1,0:T(8,128)(2,1)S(1)}, bf16[1,1536,128]{2,1,0:T(8,128)(2,1)}, u32[]{:S(2)}) copy-start(bf16[1,1536,128]{2,1,0:T(8,128)(2,1)} %param.25) | copy-start | bytes 1179652
  337.1 2.7 copy-start.2
  339.8 1.8 copy-start.6
  339.8 1.9 copy-start.7
  500.3 10.8 %copy-start.11 = (f32[128,8]{0,1:T(8,128)S(1)}, f32[128,8]{0,1:T(8,128)}, u32[]{:S(2)}) copy-start(f32[128,8]{0,1:T(8,128)} %param.33) | copy-start | bytes 12292
  500.3 49.8 %all-to-all-start.1 = ((bf16[64,32,384]{2,1,0:T(8,128)(2,1)}), bf16[64,32,384]{2,1,0:T(8,128)(2,1)S(1)}, u32[]{:S(2)}, u32[]{:S(2)}) async-start(bf16[64,32,384]{2,1,0:T(8,128)(2,1)} %bitcast.149), calls=%async_computation.1 | async-start | bytes 3145728 | tf_op jit(solution)/shard_map/all_to_all | solution.py:124
  550.1 6.9 %copy-start.1 = (bf16[384,1536]{1,0:T(8,128)(2,1)S(1)}, bf16[384,1536]{1,0:T(8,128)(2,1)}, u32[]{:S(2)}) copy-start(bf16[384,1536]{1,0:T(8,128)(2,1)} %param.23) | copy-start | bytes 3538948
Sparse Core Ops, SparseCore 0:
  130.9 34.0 all-gather.2
  420.3 62.8 reduce-scatter.3
